TPU v7x, 512 devices: a whole 4x8x8 slice. The times are simulated.
512 devices in a mesh: batch: 8 (over y), grp: 64 (over x, z, core).
Axes of the slice: x: 4, y: 8, z: 8, core: 2. Of those that a mesh axis runs over, the one named last changes fastest.
Arguments:
- amps: bfloat16 [24, 64, 1024, 128], P('batch', None, 'grp'), may hold values from -6 to 6
- cycle_inter: bfloat16 [24, 1024, 8, 128], P('batch', 'grp'), may hold values from -0.109375 to 0.109375
- k_irrep: int32 [24], replicated, may hold values from 0 to 7
- i_irrep: int32 [64], replicated, may hold values from 0 to 7
- j_irrep: int32 [8], replicated, may hold values from 0 to 7
- virt_count: int32 [8], replicated, may hold values from 64 to 128, as said below
Outputs:
- cycle_term: bfloat16 [64, 8, 1024, 128], P(None, 'batch', 'grp')
Inputs may be any that keep to these rules, and one draw needn't show every extreme that they name: `virt_count`: together the counts are 800.
All inputs are finite; a program needn't handle non-finite values.
Results may differ from a plain program's by a relative error of at most 0.013.
Values may be sent and summed in bfloat16 or wider, within the bound.
A program may use at most 64 MiB of HBM per device.

v0:
```python
import jax
import jax.numpy as jnp
from jax import lax
from jax.sharding import PartitionSpec as P


def shards(amps, cycle_inter, k_irrep, i_irrep, j_irrep, virt_count):
    k_local = amps.shape[0]
    slab_size = amps.shape[2]
    width = amps.shape[3]
    n_irrep = virt_count.shape[0]
    j_total = cycle_inter.shape[2]
    irreps = jnp.arange(n_irrep, dtype=jnp.int32)
    slot_pos = jnp.arange(width, dtype=jnp.int32)

    def count_of(labels):
        return jnp.sum(jnp.where(labels[..., None] == irreps, virt_count, 0), axis=-1)

    k_first = lax.axis_index("batch") * k_local
    k_labels = lax.dynamic_slice_in_dim(k_irrep, k_first, k_local)
    c_index = lax.axis_index("grp") * slab_size + jnp.arange(slab_size, dtype=jnp.int32)
    c_labels = c_index // width
    c_live = c_index % width < count_of(c_labels)
    a_labels = jnp.bitwise_xor(
        jnp.bitwise_xor(k_labels[:, None, None], i_irrep[None, :, None]), c_labels[None, None, :]
    )
    amp_mask = c_live[None, None, :, None] & (slot_pos < count_of(a_labels)[..., None])
    masked_amps = jnp.where(amp_mask, amps, jnp.zeros((), amps.dtype))
    b_labels = jnp.bitwise_xor(
        jnp.bitwise_xor(k_labels[:, None, None], c_labels[None, :, None]), j_irrep[None, None, :]
    )
    inter_mask = c_live[None, :, None, None] & (slot_pos < count_of(b_labels)[..., None])
    masked_inter = jnp.where(inter_mask, cycle_inter, jnp.zeros((), cycle_inter.dtype))
    sorted_amps = lax.all_to_all(masked_amps, "grp", split_axis=1, concat_axis=2, tiled=True)
    whole_inter = lax.all_gather(masked_inter, "grp", axis=1, tiled=True)
    i_count = sorted_amps.shape[1]
    i_labels = lax.dynamic_slice_in_dim(i_irrep, lax.axis_index("grp") * i_count, i_count)
    k_source = jnp.bitwise_xor(irreps[None, :], k_labels[:, None])
    amp_blocks = sorted_amps.reshape(k_local, i_count, n_irrep, width, width)
    amp_perm = jnp.take_along_axis(amp_blocks, k_source[:, None, :, None, None], axis=2)
    inter_blocks = whole_inter.reshape(k_local, n_irrep, width, j_total, width)
    inter_perm = jnp.take_along_axis(inter_blocks, k_source[:, :, None, None, None], axis=1)
    products = jnp.einsum(
        "kiqca,kqcjb->iqajb", amp_perm, inter_perm, preferred_element_type=jnp.float32
    )
    i_source = jnp.bitwise_xor(irreps[None, :], i_labels[:, None])
    partial_value = jnp.take_along_axis(products, i_source[:, :, None, None, None], axis=1)
    partial_value = jnp.transpose(partial_value, (0, 3, 1, 2, 4)).reshape(
        i_count, j_total, n_irrep * width, width
    )
    rounded = partial_value.astype(jnp.bfloat16)
    resorted = lax.all_to_all(rounded, "grp", split_axis=2, concat_axis=0, tiled=True)
    return lax.psum_scatter(
        resorted.astype(jnp.float32).astype(jnp.bfloat16), "batch", scatter_dimension=1, tiled=True
    )


def solution(mesh):
    return jax.shard_map(
        shards,
        mesh=mesh,
        in_specs=(P("batch", None, "grp", None), P("batch", "grp", None, None), P(), P(), P(), P()),
        out_specs=P(None, "batch", "grp", None),
        check_vma=False,
    )
```

profile of v0, /device:TPU:2, one launch (start us, length us, event | category | flops | bytes accessed | tf_op | source)
XLA Modules:
  0.0 233.2 jit_solution(9864530524184369395)
XLA Ops:
  6.5 0.0 copy-start
  6.5 0.0 all-gather.2.cloned.1.call-start
  6.6 0.7 dynamic_slice.7
  7.3 0.1 broadcast_xor_fusion.3
  7.4 0.7 select_reduce_fusion.2
  8.1 0.7 broadcast_xor_fusion.1
  8.8 0.8 select_reduce_fusion.1
  9.6 0.1 copy.26
  9.7 1.7 fusion.11
  11.3 0.0 all-gather.2.cloned.1.call-update
  11.4 0.7 broadcast_xor_fusion.2
  12.1 0.1 broadcast_xor_fusion
  12.2 0.8 select_reduce_fusion
  13.0 0.1 copy.27
  13.1 2.3 %fusion.8 = bf16[3,64,16,128]{3,2,0,1:T(8,128)(2,1)} fusion(bf16[3,64,16,128]{3,2,1,0:T(8,128)(2,1)} %param.6, s32[3,64,16]{2,0,1:T(4,128)S(1)} %copy.27, pred[16]{0:T(512)(128)(4,1)S(1)} %fusion.18), kind=kLoop, calls=%fused_computation.12 | loop fusion | flops 1179648 | bytes 1585168 | tf_op jit(solution)/shard_map/jit(_where)/select_n | solution.py:28
  15.4 13.9 %all-to-all-start = ((bf16[3,64,16,128]{3,2,0,1:T(8,128)(2,1)}), bf16[3,64,16,128]{3,2,0,1:T(8,128)(2,1)S(1)}, u32[]{:S(2)}, u32[]{:S(2)}) async-start(bf16[3,64,16,128]{3,2,0,1:T(8,128)(2,1)} %fusion.8), calls=%async_computation | async-start | bytes 1572864 | tf_op jit(solution)/shard_map/all_to_all | solution.py:34
  29.3 0.0 reduce-scatter.2.cloned.1.call-start
  29.3 0.1 fusion.14
  29.4 0.1 reshape.379
  29.5 0.0 copy-done
  29.5 0.6 dynamic_slice.6
  30.1 0.6 fusion.19
  30.8 0.6 compare_and_fusion
  31.4 0.1 fusion.17
  31.5 22.4 %all-to-all-done = bf16[3,64,16,128]{3,2,0,1:T(8,128)(2,1)S(1)} async-done(((bf16[3,64,16,128]{3,2,0,1:T(8,128)(2,1)}), bf16[3,64,16,128]{3,2,0,1:T(8,128)(2,1)S(1)}, u32[]{:S(2)}, u32[]{:S(2)}) %all-to-all-start) | async-done | bytes 786464 | tf_op jit(solution)/shard_map/all_to_all | solution.py:34
  53.9 0.1 copy.29
  54.0 0.8 gather_fusion.2
  54.8 47.8 %all-gather.2.cloned.1.call-done = bf16[3,1024,8,128]{3,2,1,0:T(8,128)(2,1)} async-done(((bf16[3,16,8,128]{3,2,1,0:T(8,128)(2,1)}), bf16[3,1024,8,128]{3,2,1,0:T(8,128)(2,1)}) %all-gather.2.cloned.1.call-update) | async-done | bytes 6291472 | tf_op jit(solution)/shard_map/all_gather | solution.py:35
  102.6 7.4 %gather_fusion.1 = bf16[24,128,8,128]{3,2,1,0:T(8,128)(2,1)} fusion(bf16[3,8,128,8,128]{4,3,2,1,0:T(8,128)(2,1)} %bitcast.40, s32[24]{0:T(128)S(1)} %reshape.379), kind=kCustom, calls=%fused_computation.1 | custom fusion | bytes 12583104 | tf_op jit(solution)/shard_map/jit(take_along_axis)/gather | solution.py:42
  110.0 3.4 %broadcast_select_fusion = bf16[3,8,128,8,128]{4,3,2,1,0:T(8,128)(2,1)S(1)} fusion(bf16[3,8,128,8,128]{4,3,2,1,0:T(8,128)(2,1)} %bitcast.37, pred[3,8]{1,0:T(4,128)(4,1)S(1)} %fusion.17), kind=kLoop, calls=%fused_computation.5 | loop fusion | flops 3145728 | bytes 12582936 | tf_op jit(solution)/shard_map/jit(take_along_axis)/select_n | solution.py:42
  113.4 3.5 %fusion.3 = bf16[8,128,8,128]{1,3,2,0:T(8,128)(2,1)} fusion(bf16[3,8,128,8,128]{4,3,2,1,0:T(8,128)(2,1)S(1)} %broadcast_select_fusion, bf16[3,8,128,128]{3,2,1,0:T(8,128)(2,1)S(1)} %bitcast.42, pred[3,8]{1,0:T(4,128)(4,1)S(1)} %fusion.17), kind=kOutput, calls=%fused_computation.8 | convolution fusion | flops 805699584 | bytes 9175064 | tf_op jit(solution)/shard_map/kiqca,kqcjb->iqajb/dot_general | solution.py:43
  117.0 2.5 %gather_fusion = bf16[8,128,8,128]{1,3,2,0:T(8,128)(2,1)S(1)} fusion(bf16[8,128,8,128]{1,3,2,0:T(8,128)(2,1)} %fusion.3, s32[1024]{0:T(1024)S(1)} %pad_clamp_fusion), kind=kCustom, calls=%fused_computation | custom fusion | bytes 4194336 | tf_op jit(solution)/shard_map/jit(take_along_axis)/gather | solution.py:47
  119.5 2.0 fusion.6
  121.5 3.2 %copy.40 = bf16[1,8,8,128,128]{4,1,3,2,0:T(8,128)(2,1)S(1)} copy(bf16[1,8,8,128,128]{3,4,1,2,0:T(8,128)(2,1)} %fusion.6) | data formatting | bytes 4194304 | tf_op jit(solution)/shard_map/convert_element_type | solution.py:51
  124.7 56.5 %all_to_all.27 = bf16[1,8,1024,128]{3,1,0,2:T(8,128)(2,1)S(1)} all-to-all(bf16[1,8,1024,128]{3,1,0,2:T(8,128)(2,1)S(1)} %bitcast.39), channel_id=1, replica_groups=mesh['batch'=8,'grp'=64] {'grp'}, dimensions={2} | all-to-all | bytes 4194304 | tf_op jit(solution)/shard_map/all_to_all | solution.py:52
  181.3 1.7 copy.34
  182.9 0.0 reduce-scatter.2.cloned.1.call-update
  183.0 43.4 %reduce-scatter.2.cloned.1.call-done = bf16[64,1,16,128]{3,2,0,1:T(8,128)(2,1)} async-done(((bf16[64,8,16,128]{3,2,0,1:T(8,128)(2,1)}), bf16[64,1,16,128]{3,2,0,1:T(8,128)(2,1)}) %reduce-scatter.2.cloned.1.call-update) | async-done | bytes 262160 | tf_op jit(solution)/shard_map/reduce_scatter | solution.py:53
  (3 shorter events, 0.0 us)
Async XLA Ops:
  6.5 23.0 %copy-start = (s32[64]{0:T(128)S(1)}, s32[64]{0:T(128)}, u32[]{:S(2)}) copy-start(s32[64]{0:T(128)} %param.9) | copy-start | bytes 772
  6.5 96.1 %all-gather.2.cloned.1.call-start = ((), (), s32[]{:S(2)}) async-start(), calls=%async_computation.3 | async-start | bytes 6389760 | tf_op jit(solution)/shard_map/all_gather | solution.py:35
  15.4 38.4 %all-to-all-start = ((bf16[3,64,16,128]{3,2,0,1:T(8,128)(2,1)}), bf16[3,64,16,128]{3,2,0,1:T(8,128)(2,1)S(1)}, u32[]{:S(2)}, u32[]{:S(2)}) async-start(bf16[3,64,16,128]{3,2,0,1:T(8,128)(2,1)} %fusion.8), calls=%async_computation | async-start | bytes 1572864 | tf_op jit(solution)/shard_map/all_to_all | solution.py:34
  29.3 197.1 %reduce-scatter.2.cloned.1.call-start = ((), (), s32[]{:S(2)}) async-start(), calls=%async_computation.4 | async-start | bytes 2359296 | tf_op jit(solution)/shard_map/reduce_scatter | solution.py:53
Sparse Core Ops, SparseCore 0:
  11.5 91.0 all-gather.1
  183.1 43.2 reduce-scatter.1
where the time goes:
time: 234 us; the launch traced here: 233 us
  waiting for transfers between devices  114 us (49%)
  blocking collectives  56.5 us (24%)
  local copies, waits for them, and re-layouts  17.3 us (7%)
  other arithmetic  14.8 us (6%)
  starting transfers between devices  13.9 us (6%)
  between operations  13.5 us (6%)
  matrix products  3.53 us (2%)
    all_to_all x1, blocking collectives, shards(): lax.all_to_all(rounded, 'grp', split_axis=2, concat_axis=0, tiled=True)  56.5 us
    all_gather x1, waiting for transfers between devices, shards(): whole_inter = lax.all_gather(masked_inter, 'grp', axis=1, tiled=True)  47.8 us
    reduce_scatter x1, waiting for transfers between devices, shards(): lax.psum_scatter(resorted.astype(jnp.float32).astype(jnp.bfloat16), 'batc...  43.4 us
    all_to_all x1, waiting for transfers between devices, shards(): lax.all_to_all(masked_amps, 'grp', split_axis=1, concat_axis=2, tiled=True)  22.4 us
    all_to_all x1, starting transfers between devices, shards(): lax.all_to_all(masked_amps, 'grp', split_axis=1, concat_axis=2, tiled=True)  13.9 us
    gather x2, local copies, waits for them, and re-layouts, shards(): jnp.take_along_axis(inter_blocks, k_source[:, :, None, None, None], axis=1)  7.46 us
  transfers between devices with their start and end apart: 3, of which 3 were waited for; matrix products, arithmetic and copies ran while one was open for 3% of the time, Pallas kernels for 0%

commit v1 on v0

--- a/solution.py
+++ b/solution.py
@@ -32,7 +32,16 @@
     inter_mask = c_live[None, :, None, None] & (slot_pos < count_of(b_labels)[..., None])
     masked_inter = jnp.where(inter_mask, cycle_inter, jnp.zeros((), cycle_inter.dtype))
     sorted_amps = lax.all_to_all(masked_amps, "grp", split_axis=1, concat_axis=2, tiled=True)
-    whole_inter = lax.all_gather(masked_inter, "grp", axis=1, tiled=True)
+    region_arrange = lambda in_array: jnp.concatenate(
+        lax.all_to_all(
+            jnp.stack(lax.axis_size("grp") * [in_array]),
+            axis_name="grp",
+            split_axis=0,
+            concat_axis=0,
+        ),
+        1,
+    )
+    whole_inter = region_arrange(masked_inter)
     i_count = sorted_amps.shape[1]
     i_labels = lax.dynamic_slice_in_dim(i_irrep, lax.axis_index("grp") * i_count, i_count)
     k_source = jnp.bitwise_xor(irreps[None, :], k_labels[:, None])

time: 234 us -> 339 us (1.45)
  the two profiles are of different devices: /device:TPU:2 before, /device:TPU:4 now
where the time goes in v1:
time: 339 us; the launch traced here: 338 us
  waiting for transfers between devices  198 us (58%)
  blocking collectives  57.5 us (17%)
  local copies, waits for them, and re-layouts  29.6 us (9%)
  starting transfers between devices  21.5 us (6%)
  other arithmetic  14.2 us (4%)
  between operations  13.5 us (4%)
  matrix products  3.53 us (1%)
    all_to_all x1, waiting for transfers between devices, shards(): lax.all_to_all(jnp.stack(lax.axis_size('grp') * [in_array]), axis_name='g...  134 us
    all_to_all x1, blocking collectives, shards(): lax.all_to_all(rounded, 'grp', split_axis=2, concat_axis=0, tiled=True)  57.5 us
    reduce_scatter x1, waiting for transfers between devices, shards(): lax.psum_scatter(resorted.astype(jnp.float32).astype(jnp.bfloat16), 'batc...  44.4 us
    all_to_all x1, waiting for transfers between devices, shards(): lax.all_to_all(masked_amps, 'grp', split_axis=1, concat_axis=2, tiled=True)  19.2 us
    all_to_all x1, starting transfers between devices, shards(): lax.all_to_all(masked_amps, 'grp', split_axis=1, concat_axis=2, tiled=True)  13.9 us
    all_to_all x1, local copies, waits for them, and re-layouts, shards(): lax.all_to_all(jnp.stack(lax.axis_size('grp') * [in_array]), axis_name='g...  8.08 us
    all_to_all x1, starting transfers between devices, shards(): lax.all_to_all(jnp.stack(lax.axis_size('grp') * [in_array]), axis_name='g...  7.54 us
    gather x2, local copies, waits for them, and re-layouts, shards(): jnp.take_along_axis(inter_blocks, k_source[:, :, None, None, None], axis=1)  7.46 us
  transfers between devices with their start and end apart: 3, of which 3 were waited for; matrix products, arithmetic and copies ran while one was open for 2% of the time, Pallas kernels for 0%

profile of v1, /device:TPU:4, one launch (start us, length us, event | category | flops | bytes accessed | tf_op | source)
XLA Modules:
  0.0 337.9 jit_solution(15253907489876671811)
XLA Ops:
  6.5 0.7 select_reduce_fusion.2
  7.3 0.7 dynamic_slice.7
  8.0 0.7 broadcast_xor_fusion.2
  8.8 0.1 broadcast_xor_fusion
  8.8 0.8 select_reduce_fusion
  9.6 0.1 copy.30
  9.7 2.4 fusion.8
  12.1 13.9 %all-to-all-start.1 = ((bf16[3,64,16,128]{3,2,0,1:T(8,128)(2,1)}), bf16[3,64,16,128]{3,2,0,1:T(8,128)(2,1)S(1)}, u32[]{:S(2)}, u32[]{:S(2)}) async-start(bf16[3,64,16,128]{3,2,0,1:T(8,128)(2,1)} %fusion.8), calls=%async_computation.1 | async-start | bytes 1572864 | tf_op jit(solution)/shard_map/all_to_all | solution.py:34
  26.0 0.1 broadcast_xor_fusion.3
  26.1 0.7 broadcast_xor_fusion.1
  26.8 0.8 select_reduce_fusion.1
  27.6 0.1 copy.28
  27.7 1.0 fusion.11
  28.7 19.2 %all-to-all-done.1 = bf16[3,64,16,128]{3,2,0,1:T(8,128)(2,1)S(1)} async-done(((bf16[3,64,16,128]{3,2,0,1:T(8,128)(2,1)}), bf16[3,64,16,128]{3,2,0,1:T(8,128)(2,1)S(1)}, u32[]{:S(2)}, u32[]{:S(2)}) %all-to-all-start.1) | async-done | bytes 786464 | tf_op jit(solution)/shard_map/all_to_all | solution.py:34
  47.9 4.2 %stack.2 = bf16[64,3,16,8,128]{4,3,2,1,0:T(8,128)(2,1)} broadcast(bf16[3,16,8,128]{3,2,1,0:T(8,128)(2,1)S(1)} %fusion.11), dimensions={1,2,3,4} | broadcast | bytes 6389760 | tf_op jit(solution)/shard_map/stack | solution.py:37
  52.2 0.0 copy-start
  52.2 7.5 %all-to-all-start = ((bf16[64,3,16,8,128]{4,3,2,1,0:T(8,128)(2,1)}), bf16[64,3,16,8,128]{4,3,2,1,0:T(8,128)(2,1)}, u32[]{:S(2)}, u32[]{:S(2)}) async-start(bf16[64,3,16,8,128]{4,3,2,1,0:T(8,128)(2,1)} %stack.2), calls=%async_computation | async-start | bytes 12582912 | tf_op jit(solution)/shard_map/all_to_all | solution.py:36
  59.7 0.0 reduce-scatter.2.cloned.1.call-start
  59.8 0.1 fusion.14
  59.9 0.1 reshape.381
  59.9 0.0 copy-done
  59.9 0.6 dynamic_slice.6
  60.5 0.6 fusion.19
  61.2 0.7 compare_and_fusion
  61.9 0.1 fusion.17
  61.9 0.1 copy.32
  62.1 0.8 gather_fusion.2
  62.8 134.3 %all-to-all-done = bf16[64,3,16,8,128]{4,3,2,1,0:T(8,128)(2,1)} async-done(((bf16[64,3,16,8,128]{4,3,2,1,0:T(8,128)(2,1)}), bf16[64,3,16,8,128]{4,3,2,1,0:T(8,128)(2,1)}, u32[]{:S(2)}, u32[]{:S(2)}) %all-to-all-start) | async-done | bytes 6291488 | tf_op jit(solution)/shard_map/all_to_all | solution.py:36
  197.2 8.1 %copy.29 = bf16[64,3,16,8,128]{4,3,2,0,1:T(8,128)(2,1)} copy(bf16[64,3,16,8,128]{4,3,2,1,0:T(8,128)(2,1)} %all-to-all-done) | data formatting | bytes 12582912 | tf_op jit(solution)/shard_map/all_to_all | solution.py:36
  205.3 7.4 %gather_fusion.1 = bf16[24,128,8,128]{3,2,1,0:T(8,128)(2,1)} fusion(bf16[3,8,128,8,128]{4,3,2,1,0:T(8,128)(2,1)} %bitcast.39, s32[24]{0:T(128)S(1)} %reshape.381), kind=kCustom, calls=%fused_computation.1 | custom fusion | bytes 12583104 | tf_op jit(solution)/shard_map/jit(take_along_axis)/gather | solution.py:51
  212.6 3.4 %broadcast_select_fusion = bf16[3,8,128,8,128]{4,3,2,1,0:T(8,128)(2,1)S(1)} fusion(bf16[3,8,128,8,128]{4,3,2,1,0:T(8,128)(2,1)} %bitcast.40, pred[3,8]{1,0:T(4,128)(4,1)S(1)} %fusion.17), kind=kLoop, calls=%fused_computation.5 | loop fusion | flops 3145728 | bytes 12582936 | tf_op jit(solution)/shard_map/jit(take_along_axis)/select_n | solution.py:51
  216.1 3.5 %fusion.3 = bf16[8,128,8,128]{1,3,2,0:T(8,128)(2,1)} fusion(bf16[3,8,128,8,128]{4,3,2,1,0:T(8,128)(2,1)S(1)} %broadcast_select_fusion, bf16[3,8,128,128]{3,2,1,0:T(8,128)(2,1)S(1)} %bitcast.44, pred[3,8]{1,0:T(4,128)(4,1)S(1)} %fusion.17), kind=kOutput, calls=%fused_computation.8 | convolution fusion | flops 805699584 | bytes 9175064 | tf_op jit(solution)/shard_map/kiqca,kqcjb->iqajb/dot_general | solution.py:52
  219.6 2.5 gather_fusion
  222.2 2.0 fusion.6
  224.2 3.2 copy.43
  227.4 57.5 %all_to_all.32 = bf16[1,8,1024,128]{3,1,0,2:T(8,128)(2,1)S(1)} all-to-all(bf16[1,8,1024,128]{3,1,0,2:T(8,128)(2,1)S(1)} %bitcast.42), channel_id=1, replica_groups=mesh['batch'=8,'grp'=64] {'grp'}, dimensions={2} | all-to-all | bytes 4194304 | tf_op jit(solution)/shard_map/all_to_all | solution.py:61
  285.0 1.7 copy.37
  286.7 0.0 reduce-scatter.2.cloned.1.call-update
  286.7 44.4 %reduce-scatter.2.cloned.1.call-done = bf16[64,1,16,128]{3,2,0,1:T(8,128)(2,1)} async-done(((bf16[64,8,16,128]{3,2,0,1:T(8,128)(2,1)}), bf16[64,1,16,128]{3,2,0,1:T(8,128)(2,1)}) %reduce-scatter.2.cloned.1.call-update) | async-done | bytes 262160 | tf_op jit(solution)/shard_map/reduce_scatter | solution.py:62
  (3 shorter events, 0.0 us)
Async XLA Ops:
  12.1 35.8 %all-to-all-start.1 = ((bf16[3,64,16,128]{3,2,0,1:T(8,128)(2,1)}), bf16[3,64,16,128]{3,2,0,1:T(8,128)(2,1)S(1)}, u32[]{:S(2)}, u32[]{:S(2)}) async-start(bf16[3,64,16,128]{3,2,0,1:T(8,128)(2,1)} %fusion.8), calls=%async_computation.1 | async-start | bytes 1572864 | tf_op jit(solution)/shard_map/all_to_all | solution.py:34
  52.2 7.8 %copy-start = (s32[64]{0:T(128)S(1)}, s32[64]{0:T(128)}, u32[]{:S(2)}) copy-start(s32[64]{0:T(128)} %param.9) | copy-start | bytes 772
  52.2 145.0 %all-to-all-start = ((bf16[64,3,16,8,128]{4,3,2,1,0:T(8,128)(2,1)}), bf16[64,3,16,8,128]{4,3,2,1,0:T(8,128)(2,1)}, u32[]{:S(2)}, u32[]{:S(2)}) async-start(bf16[64,3,16,8,128]{4,3,2,1,0:T(8,128)(2,1)} %stack.2), calls=%async_computation | async-start | bytes 12582912 | tf_op jit(solution)/shard_map/all_to_all | solution.py:36
  59.7 271.4 %reduce-scatter.2.cloned.1.call-start = ((), (), s32[]{:S(2)}) async-start(), calls=%async_computation.4 | async-start | bytes 2359296 | tf_op jit(solution)/shard_map/reduce_scatter | solution.py:62
Sparse Core Ops, SparseCore 0:
  286.8 44.2 reduce-scatter.1
